TPU v7x, 32 devices: a whole 2x2x4 slice. The times are simulated.
32 devices in a mesh: lon: 2 (over x), lat: 16 (over z, y, core).
Axes of the slice: x: 2, y: 2, z: 4, core: 2. Of those that a mesh axis runs over, the one named last changes fastest.
Arguments:
- state: bfloat16 [1, 128, 256, 128], P(None, 'lat', 'lon'), may hold values from -6 to 6
- mix_weight: bfloat16 [128, 2, 128, 128], P('lat'), may hold values from -0.375 to 0.375
- skip_weight: bfloat16 [128, 128], replicated, may hold values from -0.5 to 0.5
Outputs:
- output: bfloat16 [1, 128, 256, 128], P(None, 'lat', 'lon')
All inputs are finite; a program needn't handle non-finite values.
Results may differ from a plain program's by a relative error of at most 0.008.
Values may be sent and summed in bfloat16 or wider, within the bound.
A program may use at most 64 MiB of HBM per device.

v0:
```python
import math
import jax
import jax.numpy as jnp
from jax import lax
from jax.sharding import PartitionSpec as P

rescale_limit = 1e18
log_rescale = 18.0 * math.log(10.0)


def lat_geometry(lat_count):
    positions = jnp.arange(lat_count, dtype=jnp.float32)
    colatitude = jnp.pi * (positions + 0.5) / lat_count
    return (jnp.cos(colatitude), jnp.sin(colatitude))


def fourier_tables(lon_count, mode_count):
    lon_index = jnp.arange(lon_count, dtype=jnp.int32)[:, None]
    mode_index = jnp.arange(mode_count, dtype=jnp.int32)[None, :]
    angles = (lon_index * mode_index % lon_count).astype(jnp.float32) * (2.0 * math.pi / lon_count)
    norming = 1.0 / math.sqrt(lon_count)
    paired = jnp.stack([jnp.cos(angles), -jnp.sin(angles)], axis=2) * norming
    weight = jnp.where(mode_index == 0, 1.0, 2.0)[:, :, None]
    forward = paired.reshape(lon_count, 2 * mode_count).astype(jnp.bfloat16)
    backward = (paired * weight).reshape(lon_count, 2 * mode_count).astype(jnp.bfloat16)
    return (forward, backward)


def legendre_tables(mode_ids, lat_count, degrees):
    cosine, sine_values = lat_geometry(lat_count)
    count = mode_ids.shape[0]
    layout = (1, lat_count // 128, 128)
    orders = mode_ids.astype(jnp.float32)[:, None]
    counter = jnp.arange(1, degrees + 1, dtype=jnp.float32)
    halves = 0.5 * jnp.log((2.0 * counter + 1.0) / (2.0 * counter))
    summed = jnp.sum(
        jnp.where(counter[None, :] <= orders, halves[None, :], jnp.float32(0.0)),
        axis=1,
        keepdims=True,
    )
    log_start = 0.5 * jnp.log(jnp.float32(0.5)) + summed + orders * jnp.log(sine_values)[None, :]
    log_start = log_start.reshape((count,) + layout[1:])
    orders = orders.reshape(count, 1, 1)
    cosine = cosine.reshape(layout)
    sine_values = sine_values.reshape(layout)
    analysis_scale = math.pi / math.sqrt(lat_count)
    synthesis_scale = 1.0 / math.sqrt(degrees)
    zeros = jnp.zeros((count,) + layout[1:], jnp.float32)

    def advance(carry, level_index):
        previous, earlier, exponent = carry
        level = level_index.astype(jnp.float32)
        ratio_a = jnp.sqrt(
            jnp.maximum(4.0 * level * level - 1.0, 0.0)
            / jnp.maximum(level * level - orders * orders, 1.0)
        )
        below = level - 1.0
        ratio_b = jnp.sqrt(
            jnp.maximum(below * below - orders * orders, 0.0)
            / jnp.maximum(4.0 * below * below - 1.0, 1.0)
        )
        raised = ratio_a * (cosine * previous - ratio_b * earlier)
        at_start = level == orders
        current = jnp.where(at_start, 1.0, jnp.where(level > orders, raised, 0.0))
        exponent = jnp.where(at_start, log_start, exponent)
        oversize = jnp.abs(current) > rescale_limit
        factor = jnp.where(oversize, 1.0 / rescale_limit, 1.0)
        earlier = previous * factor
        previous = current * factor
        exponent = exponent + jnp.where(oversize, log_rescale, 0.0)
        value = previous * jnp.exp(exponent)
        analysis_row = (value * analysis_scale * sine_values).astype(jnp.bfloat16)
        synthesis_row = (value * synthesis_scale).astype(jnp.bfloat16)
        return ((previous, earlier, exponent), (analysis_row, synthesis_row))

    levels = jnp.arange(degrees, dtype=jnp.int32)
    outputs = lax.scan(advance, (zeros, zeros, zeros), levels, unroll=32)[1]
    analysis = outputs[0].reshape(degrees, count, lat_count)
    synthesis = outputs[1].reshape(degrees, count, lat_count)
    return (analysis, synthesis)


def mixing_blocks(mix_weight):
    real_part = mix_weight[:, 0]
    imag_part = mix_weight[:, 1]
    upper = jnp.concatenate([real_part, imag_part], axis=2)
    lower = jnp.concatenate([-imag_part, real_part], axis=2)
    return jnp.concatenate([upper, lower], axis=1)


def shards(state, mix_weight, skip_weight):
    samples, lat_dev, lon_dev, channels = state.shape
    lon_groups = lax.axis_size("lon")
    lat_groups = lax.axis_size("lat")
    lon_count = lon_dev * lon_groups
    lat_count = lat_dev * lat_groups
    mode_count = lon_count // 2
    lon_modes = mode_count // lon_groups
    own_modes = lon_modes // lat_groups
    forward, backward = fourier_tables(lon_count, mode_count)
    first_mode = lax.axis_index("lon") * lon_modes + lax.axis_index("lat") * own_modes
    mode_ids = first_mode + jnp.arange(own_modes, dtype=jnp.int32)
    analysis, synthesis = legendre_tables(mode_ids, lat_count, mode_count)
    block_weight = mixing_blocks(mix_weight)
    received = lax.all_to_all(state, "lon", split_axis=1, concat_axis=2, tiled=True)
    items = received.shape[0]
    row_count = received.shape[1]
    spectra = jnp.einsum(
        "sjkc,kq->sjqc", received, forward, preferred_element_type=jnp.float32
    ).astype(jnp.bfloat16)
    spectra = spectra.reshape(items, row_count, lon_groups, 2 * lon_modes, channels)
    spectra = lax.all_to_all(spectra, "lon", split_axis=2, concat_axis=1, tiled=True)
    spectrum = spectra.reshape(items, lat_dev, 2 * lon_modes, channels)
    received = lax.all_to_all(spectrum, "lat", split_axis=2, concat_axis=1, tiled=True)
    items = received.shape[0]
    pieces = received.reshape(items, lat_count, own_modes, 2, channels)
    coeffs = jnp.einsum(
        "lij,sjirc->slirc", analysis, pieces, preferred_element_type=jnp.float32
    ).astype(jnp.bfloat16)
    coeffs = coeffs.reshape(items, mode_count, 2 * own_modes, channels)
    coefficients = lax.all_to_all(coeffs, "lat", split_axis=1, concat_axis=2, tiled=True)
    deg_dev = coefficients.shape[1]
    paired = coefficients.reshape(samples, deg_dev, lon_modes, 2 * channels)
    mixed = jnp.einsum(
        "slix,lxy->sliy", paired, block_weight, preferred_element_type=jnp.float32
    ).astype(jnp.bfloat16)
    mixed = mixed.reshape(samples, deg_dev, 2 * lon_modes, channels)
    received = lax.all_to_all(mixed, "lat", split_axis=2, concat_axis=1, tiled=True)
    items = received.shape[0]
    pieces = received.reshape(items, mode_count, own_modes, 2 * channels)
    gridded = jnp.einsum(
        "lij,sliy->sjiy", synthesis, pieces, preferred_element_type=jnp.float32
    ).astype(jnp.bfloat16)
    gridded = gridded.reshape(items, lat_count, 2 * own_modes, channels)
    grid_modes = lax.all_to_all(gridded, "lat", split_axis=1, concat_axis=2, tiled=True)
    grid_modes = grid_modes.reshape(samples, lat_dev, 1, 2 * lon_modes, channels)
    received = lax.all_to_all(grid_modes, "lon", split_axis=1, concat_axis=2, tiled=True)
    items = received.shape[0]
    row_count = received.shape[1]
    spectra = received.reshape(items, row_count, 2 * mode_count, channels)
    values = jnp.einsum(
        "sjqc,kq->sjkc", spectra, backward, preferred_element_type=jnp.float32
    ).astype(jnp.bfloat16)
    spectral = lax.all_to_all(values, "lon", split_axis=2, concat_axis=1, tiled=True)
    local_term = jnp.einsum("sjkc,cd->sjkd", state, skip_weight, preferred_element_type=jnp.float32)
    return jax.nn.gelu(spectral.astype(jnp.float32) + local_term).astype(jnp.bfloat16)


def solution(mesh):
    placed = (P(None, "lat", "lon", None), P("lat", None, None, None), P())
    return jax.shard_map(
        shards, mesh=mesh, in_specs=placed, out_specs=P(None, "lat", "lon", None), check_vma=False
    )
```

profile of v0, /device:TPU:0, one launch (start us, length us, event | category | flops | bytes accessed | tf_op | source)
XLA Modules:
  0.0 206.9 jit_solution(11996657977514319588)
XLA Ops:
  0.0 4.4 %all-to-all-start = ((bf16[1,8,128,128]{3,2,0,1:T(8,128)(2,1)}), bf16[1,8,128,128]{3,2,0,1:T(8,128)(2,1)S(1)}, u32[]{:S(2)}, u32[]{:S(2)}) async-start(bf16[1,8,128,128]{3,2,0,1:T(8,128)(2,1)} %bitcast.1187), calls=%async_computation | async-start | bytes 524288 | tf_op jit(solution)/shard_map/all_to_all | solution.py:105
  4.4 0.5 sine_negate_fusion
  5.0 0.1 copy.339
  5.2 0.2 select_reduce_fusion
  5.4 4.8 %all-to-all-done = bf16[1,8,128,128]{3,2,0,1:T(8,128)(2,1)S(1)} async-done(((bf16[1,8,128,128]{3,2,0,1:T(8,128)(2,1)}), bf16[1,8,128,128]{3,2,0,1:T(8,128)(2,1)S(1)}, u32[]{:S(2)}, u32[]{:S(2)}) %all-to-all-start) | async-done | bytes 262176 | tf_op jit(solution)/shard_map/all_to_all | solution.py:105
  10.3 0.2 convolution_convert_fusion.4
  10.5 0.7 copy.342
  11.2 3.4 %all-to-all-start.1 = ((bf16[1,4,2,128,128]{4,3,1,0,2:T(8,128)(2,1)}), bf16[1,4,2,128,128]{4,3,1,0,2:T(8,128)(2,1)S(1)}, u32[]{:S(2)}, u32[]{:S(2)}) async-start(bf16[1,4,2,128,128]{4,3,1,0,2:T(8,128)(2,1)} %copy.342), calls=%async_computation.1 | async-start | bytes 524288 | tf_op jit(solution)/shard_map/all_to_all | solution.py:112
  14.8 5.1 %all-to-all-done.1 = bf16[1,4,2,128,128]{4,3,1,0,2:T(8,128)(2,1)S(1)} async-done(((bf16[1,4,2,128,128]{4,3,1,0,2:T(8,128)(2,1)}), bf16[1,4,2,128,128]{4,3,1,0,2:T(8,128)(2,1)S(1)}, u32[]{:S(2)}, u32[]{:S(2)}) %all-to-all-start.1) | async-done | bytes 262176 | tf_op jit(solution)/shard_map/all_to_all | solution.py:112
  19.8 0.9 copy.343
  20.7 6.2 %all-to-all-start.2 = ((bf16[1,8,128,128]{3,1,0,2:T(8,128)(2,1)}), bf16[1,8,128,128]{3,1,0,2:T(8,128)(2,1)S(1)}, u32[]{:S(2)}, u32[]{:S(2)}) async-start(bf16[1,8,128,128]{3,1,0,2:T(8,128)(2,1)} %copy.343), calls=%async_computation.2 | async-start | bytes 524288 | tf_op jit(solution)/shard_map/all_to_all | solution.py:114
  26.9 115.9 %while.25 = (s32[]{:T(128)}, f32[4,1,128]{2,0,1:T(4,128)S(1)}, f32[4,1,128]{2,0,1:T(4,128)S(1)}, f32[4,1,128]{2,0,1:T(4,128)S(1)}, bf16[4,32,4,1,128]{4,2,1,3,0:...) while((s32[]{:T(128)}, f32[4,1,128]{2,0,1:T(4,128)S(1)}, ...), condition=%wide.region_2.3_spmd.clone.clone.clone.clone, body=%wide.region_1.2_spmd.clone.clone.clone.clone.sunk | while | flops 619265 | bytes 824448 | solution.py:77
  27.0 0.7 fusion.393
  36.9 0.7 fusion.392
  51.6 0.1 constant_dynamic-update-slice_fusion.133
  51.8 0.1 constant_dynamic-update-slice_fusion.135
  52.1 0.1 constant_dynamic-update-slice_fusion.139
  52.3 0.1 constant_dynamic-update-slice_fusion.141
  52.9 0.1 constant_dynamic-update-slice_fusion.147
  53.5 0.1 constant_dynamic-update-slice_fusion.153
  54.0 0.1 constant_dynamic-update-slice_fusion.159
  56.0 0.7 fusion.393
  65.9 0.7 fusion.392
  80.3 0.1 constant_dynamic-update-slice_fusion.131
  80.9 0.1 constant_dynamic-update-slice_fusion.137
  81.5 0.1 constant_dynamic-update-slice_fusion.143
  82.1 0.1 constant_dynamic-update-slice_fusion.149
  82.3 0.1 constant_dynamic-update-slice_fusion.151
  82.6 0.1 constant_dynamic-update-slice_fusion.155
  82.8 0.1 constant_dynamic-update-slice_fusion.157
  85.0 0.7 fusion.393
  94.9 0.7 fusion.392
  109.5 0.1 constant_dynamic-update-slice_fusion.133
  109.7 0.1 constant_dynamic-update-slice_fusion.135
  110.1 0.1 constant_dynamic-update-slice_fusion.139
  110.3 0.1 constant_dynamic-update-slice_fusion.141
  110.6 0.1 constant_dynamic-update-slice_fusion.145
  110.8 0.1 constant_dynamic-update-slice_fusion.147
  111.4 0.1 constant_dynamic-update-slice_fusion.153
  112.0 0.1 constant_dynamic-update-slice_fusion.159
  113.9 0.7 fusion.393
  123.8 0.7 fusion.392
  138.3 0.1 constant_dynamic-update-slice_fusion.131
  142.8 0.2 copy.345
  143.0 0.3 convolution_convert_fusion.3
  143.3 0.9 copy.348
  144.2 6.0 %all-to-all-start.3 = ((bf16[1,128,8,128]{3,2,0,1:T(8,128)(2,1)}), bf16[1,128,8,128]{3,2,0,1:T(8,128)(2,1)S(1)}, u32[]{:S(2)}, u32[]{:S(2)}) async-start(bf16[1,128,8,128]{3,2,0,1:T(8,128)(2,1)} %copy.348), calls=%async_computation.3 | async-start | bytes 524288 | tf_op jit(solution)/shard_map/all_to_all | solution.py:121
  150.3 9.9 %all-to-all-done.3 = bf16[1,128,8,128]{3,2,0,1:T(8,128)(2,1)S(1)} async-done(((bf16[1,128,8,128]{3,2,0,1:T(8,128)(2,1)}), bf16[1,128,8,128]{3,2,0,1:T(8,128)(2,1)S(1)}, u32[]{:S(2)}, u32[]{:S(2)}) %all-to-all-start.3) | async-done | bytes 262176 | tf_op jit(solution)/shard_map/all_to_all | solution.py:121
  160.4 0.3 fusion.298
  160.8 0.2 copy.350
  160.9 12.7 %all_to_all.114 = bf16[1,8,128,128]{3,1,0,2:T(8,128)(2,1)S(1)} all-to-all(bf16[1,8,128,128]{3,1,0,2:T(8,128)(2,1)S(1)} %copy.350), channel_id=1, replica_groups=mesh['lon'=2,'lat'=16] {'lat'}, dimensions={2} | all-to-all | bytes 524288 | tf_op jit(solution)/shard_map/all_to_all | solution.py:128
  173.7 0.2 reshape.2627
  173.9 0.3 convolution_convert_fusion.2
  174.2 0.2 copy.355
  174.4 12.7 %all_to_all.115 = bf16[1,128,8,128]{3,2,0,1:T(8,128)(2,1)S(1)} all-to-all(bf16[1,128,8,128]{3,2,0,1:T(8,128)(2,1)S(1)} %copy.355), channel_id=1, replica_groups=mesh['lon'=2,'lat'=16] {'lat'}, dimensions={1} | all-to-all | bytes 524288 | tf_op jit(solution)/shard_map/all_to_all | solution.py:135
  187.1 0.8 copy.379
  187.8 3.4 %all-to-all-start.6 = ((bf16[1,8,1,128,128]{4,3,2,0,1:T(8,128)(2,1)}), bf16[1,8,1,128,128]{4,3,2,0,1:T(8,128)(2,1)S(1)}, u32[]{:S(2)}, u32[]{:S(2)}) async-start(bf16[1,8,1,128,128]{4,3,2,0,1:T(8,128)(2,1)} %bitcast.715), calls=%async_computation.6 | async-start | bytes 524288 | tf_op jit(solution)/shard_map/all_to_all | solution.py:137
  191.3 0.1 copy.336
  191.5 5.3 %all-to-all-done.6 = bf16[1,8,1,128,128]{4,3,2,0,1:T(8,128)(2,1)S(1)} async-done(((bf16[1,8,1,128,128]{4,3,2,0,1:T(8,128)(2,1)}), bf16[1,8,1,128,128]{4,3,2,0,1:T(8,128)(2,1)S(1)}, u32[]{:S(2)}, u32[]{:S(2)}) %all-to-all-start.6) | async-done | bytes 262176 | tf_op jit(solution)/shard_map/all_to_all | solution.py:137
  196.8 0.3 fusion.297
  197.1 0.2 copy.360
  197.3 7.6 %all_to_all.116 = bf16[1,4,256,128]{3,1,0,2:T(4,128)(2,1)S(1)} all-to-all(bf16[1,4,256,128]{3,1,0,2:T(4,128)(2,1)S(1)} %copy.360), channel_id=1, replica_groups=mesh['lon'=2,'lat'=16] {'lon'}, dimensions={2} | all-to-all | bytes 524288 | tf_op jit(solution)/shard_map/all_to_all | solution.py:144
  204.9 0.9 copy-done.2
  205.8 1.1 fusion.314
  (796 shorter events, 24.5 us)
Async XLA Ops:
  0.0 204.9 %copy-start = (bf16[128,128]{1,0:T(8,128)(2,1)S(1)}, bf16[128,128]{1,0:T(8,128)(2,1)}, u32[]{:S(2)}) copy-start(bf16[128,128]{1,0:T(8,128)(2,1)} %param.7) | copy-start | bytes 98308
  0.0 10.2 %all-to-all-start = ((bf16[1,8,128,128]{3,2,0,1:T(8,128)(2,1)}), bf16[1,8,128,128]{3,2,0,1:T(8,128)(2,1)S(1)}, u32[]{:S(2)}, u32[]{:S(2)}) async-start(bf16[1,8,128,128]{3,2,0,1:T(8,128)(2,1)} %bitcast.1187), calls=%async_computation | async-start | bytes 524288 | tf_op jit(solution)/shard_map/all_to_all | solution.py:105
  11.2 8.6 %all-to-all-start.1 = ((bf16[1,4,2,128,128]{4,3,1,0,2:T(8,128)(2,1)}), bf16[1,4,2,128,128]{4,3,1,0,2:T(8,128)(2,1)S(1)}, u32[]{:S(2)}, u32[]{:S(2)}) async-start(bf16[1,4,2,128,128]{4,3,1,0,2:T(8,128)(2,1)} %copy.342), calls=%async_computation.1 | async-start | bytes 524288 | tf_op jit(solution)/shard_map/all_to_all | solution.py:112
  20.7 122.1 %all-to-all-start.2 = ((bf16[1,8,128,128]{3,1,0,2:T(8,128)(2,1)}), bf16[1,8,128,128]{3,1,0,2:T(8,128)(2,1)S(1)}, u32[]{:S(2)}, u32[]{:S(2)}) async-start(bf16[1,8,128,128]{3,1,0,2:T(8,128)(2,1)} %copy.343), calls=%async_computation.2 | async-start | bytes 524288 | tf_op jit(solution)/shard_map/all_to_all | solution.py:114
  143.3 6.9 %copy-start.1 = (bf16[8,2,128,128]{3,2,1,0:T(8,128)(2,1)S(1)}, bf16[8,2,128,128]{3,2,1,0:T(8,128)(2,1)}, u32[]{:S(2)}) copy-start(bf16[8,2,128,128]{3,2,1,0:T(8,128)(2,1)} %param.6) | copy-start | bytes 1572868
  144.2 16.0 %all-to-all-start.3 = ((bf16[1,128,8,128]{3,2,0,1:T(8,128)(2,1)}), bf16[1,128,8,128]{3,2,0,1:T(8,128)(2,1)S(1)}, u32[]{:S(2)}, u32[]{:S(2)}) async-start(bf16[1,128,8,128]{3,2,0,1:T(8,128)(2,1)} %copy.348), calls=%async_computation.3 | async-start | bytes 524288 | tf_op jit(solution)/shard_map/all_to_all | solution.py:121
  187.8 9.0 %all-to-all-start.6 = ((bf16[1,8,1,128,128]{4,3,2,0,1:T(8,128)(2,1)}), bf16[1,8,1,128,128]{4,3,2,0,1:T(8,128)(2,1)S(1)}, u32[]{:S(2)}, u32[]{:S(2)}) async-start(bf16[1,8,1,128,128]{4,3,2,0,1:T(8,128)(2,1)} %bitcast.715), calls=%async_computation.6 | async-start | bytes 524288 | tf_op jit(solution)/shard_map/all_to_all | solution.py:137
  204.9 1.0 copy-start.2
where the time goes:
time: 209 us; the launch traced here: 207 us
  loops' own time  84.2 us (40%)
  blocking collectives  32.9 us (16%)
  other arithmetic  26.6 us (13%)
  waiting for transfers between devices  25.1 us (12%)
  starting transfers between devices  23.4 us (11%)
  local copies, waits for them, and re-layouts  11.8 us (6%)
  matrix products  2.38 us (1%)
    another operation x1, loops' own time, legendre_tables(): outputs = lax.scan(advance, (zeros, zeros, zeros), levels, unroll=32)[1]  84.2 us
    while x248, other arithmetic  18 us
    all_to_all x1, blocking collectives, shards(): lax.all_to_all(mixed, 'lat', split_axis=2, concat_axis=1, tiled=True)  12.7 us
    all_to_all x1, blocking collectives, shards(): lax.all_to_all(gridded, 'lat', split_axis=1, concat_axis=2, tiled=True)  12.7 us
    all_to_all x1, waiting for transfers between devices, shards(): lax.all_to_all(coeffs, 'lat', split_axis=1, concat_axis=2, tiled=True)  9.91 us
    all_to_all x1, blocking collectives, shards(): lax.all_to_all(values, 'lon', split_axis=2, concat_axis=1, tiled=True)  7.56 us
    all_to_all x1, starting transfers between devices, shards(): lax.all_to_all(spectrum, 'lat', split_axis=2, concat_axis=1, tiled=True)  6.19 us
    all_to_all x1, starting transfers between devices, shards(): lax.all_to_all(coeffs, 'lat', split_axis=1, concat_axis=2, tiled=True)  6 us
  transfers between devices with their start and end apart: 5, of which 4 were waited for; matrix products, arithmetic and copies ran while one was open for 16% of the time, Pallas kernels for 0%

commit v1 on v0

--- a/solution.py
+++ b/solution.py
@@ -125,7 +125,9 @@
         "slix,lxy->sliy", paired, block_weight, preferred_element_type=jnp.float32
     ).astype(jnp.bfloat16)
     mixed = mixed.reshape(samples, deg_dev, 2 * lon_modes, channels)
-    received = lax.all_to_all(mixed, "lat", split_axis=2, concat_axis=1, tiled=True)
+    frame_out = jnp.split(mixed, lax.axis_size("lat"), axis=2)
+    r2 = lax.all_to_all(jnp.stack(frame_out), axis_name="lat", split_axis=0, concat_axis=0)
+    received = jnp.concatenate(r2, 1)
     items = received.shape[0]
     pieces = received.reshape(items, mode_count, own_modes, 2 * channels)
     gridded = jnp.einsum(

time: 209 us -> 209 us (level)
  no operation moved by 1% of the time
where the time goes in v1:
time: 209 us; the launch traced here: 207 us
  loops' own time  84.2 us (40%)
  blocking collectives  32.9 us (16%)
  other arithmetic  26.6 us (13%)
  waiting for transfers between devices  25.1 us (12%)
  starting transfers between devices  23.4 us (11%)
  local copies, waits for them, and re-layouts  11.8 us (6%)
  matrix products  2.38 us (1%)
    another operation x1, loops' own time, legendre_tables(): outputs = lax.scan(advance, (zeros, zeros, zeros), levels, unroll=32)[1]  84.2 us
    while x248, other arithmetic  18 us
    all_to_all x1, blocking collectives, shards(): lax.all_to_all(gridded, 'lat', split_axis=1, concat_axis=2, tiled=True)  12.7 us
    all_to_all x1, blocking collectives, shards(): lax.all_to_all(jnp.stack(frame_out), axis_name='lat', split_axis=0, conca...  12.7 us
    all_to_all x1, waiting for transfers between devices, shards(): lax.all_to_all(coeffs, 'lat', split_axis=1, concat_axis=2, tiled=True)  9.91 us
    all_to_all x1, blocking collectives, shards(): lax.all_to_all(values, 'lon', split_axis=2, concat_axis=1, tiled=True)  7.56 us
    all_to_all x1, starting transfers between devices, shards(): lax.all_to_all(spectrum, 'lat', split_axis=2, concat_axis=1, tiled=True)  6.19 us
    all_to_all x1, starting transfers between devices, shards(): lax.all_to_all(coeffs, 'lat', split_axis=1, concat_axis=2, tiled=True)  6 us
  transfers between devices with their start and end apart: 5, of which 4 were waited for; matrix products, arithmetic and copies ran while one was open for 16% of the time, Pallas kernels for 0%

profile of v1, /device:TPU:0, one launch (start us, length us, event | category | flops | bytes accessed | tf_op | source)
XLA Modules:
  0.0 206.9 jit_solution(11381531959015944369)
XLA Ops:
  0.0 4.4 %all-to-all-start = ((bf16[1,8,128,128]{3,2,0,1:T(8,128)(2,1)}), bf16[1,8,128,128]{3,2,0,1:T(8,128)(2,1)S(1)}, u32[]{:S(2)}, u32[]{:S(2)}) async-start(bf16[1,8,128,128]{3,2,0,1:T(8,128)(2,1)} %bitcast.1245), calls=%async_computation | async-start | bytes 524288 | tf_op jit(solution)/shard_map/all_to_all | solution.py:105
  4.4 0.5 sine_negate_fusion
  5.0 0.1 copy.297
  5.2 0.2 select_reduce_fusion
  5.4 4.8 %all-to-all-done = bf16[1,8,128,128]{3,2,0,1:T(8,128)(2,1)S(1)} async-done(((bf16[1,8,128,128]{3,2,0,1:T(8,128)(2,1)}), bf16[1,8,128,128]{3,2,0,1:T(8,128)(2,1)S(1)}, u32[]{:S(2)}, u32[]{:S(2)}) %all-to-all-start) | async-done | bytes 262176 | tf_op jit(solution)/shard_map/all_to_all | solution.py:105
  10.3 0.2 convolution_convert_fusion.4
  10.5 0.7 copy.300
  11.2 3.4 %all-to-all-start.1 = ((bf16[1,4,2,128,128]{4,3,1,0,2:T(8,128)(2,1)}), bf16[1,4,2,128,128]{4,3,1,0,2:T(8,128)(2,1)S(1)}, u32[]{:S(2)}, u32[]{:S(2)}) async-start(bf16[1,4,2,128,128]{4,3,1,0,2:T(8,128)(2,1)} %copy.300), calls=%async_computation.1 | async-start | bytes 524288 | tf_op jit(solution)/shard_map/all_to_all | solution.py:112
  14.8 5.1 %all-to-all-done.1 = bf16[1,4,2,128,128]{4,3,1,0,2:T(8,128)(2,1)S(1)} async-done(((bf16[1,4,2,128,128]{4,3,1,0,2:T(8,128)(2,1)}), bf16[1,4,2,128,128]{4,3,1,0,2:T(8,128)(2,1)S(1)}, u32[]{:S(2)}, u32[]{:S(2)}) %all-to-all-start.1) | async-done | bytes 262176 | tf_op jit(solution)/shard_map/all_to_all | solution.py:112
  19.8 0.9 copy.301
  20.7 6.2 %all-to-all-start.2 = ((bf16[1,8,128,128]{3,1,0,2:T(8,128)(2,1)}), bf16[1,8,128,128]{3,1,0,2:T(8,128)(2,1)S(1)}, u32[]{:S(2)}, u32[]{:S(2)}) async-start(bf16[1,8,128,128]{3,1,0,2:T(8,128)(2,1)} %copy.301), calls=%async_computation.2 | async-start | bytes 524288 | tf_op jit(solution)/shard_map/all_to_all | solution.py:114
  26.9 115.9 %while.25 = (s32[]{:T(128)}, f32[4,1,128]{2,0,1:T(4,128)S(1)}, f32[4,1,128]{2,0,1:T(4,128)S(1)}, f32[4,1,128]{2,0,1:T(4,128)S(1)}, bf16[4,32,4,1,128]{4,2,1,3,0:...) while((s32[]{:T(128)}, f32[4,1,128]{2,0,1:T(4,128)S(1)}, ...), condition=%wide.region_2.3_spmd.clone.clone.clone.clone, body=%wide.region_1.2_spmd.clone.clone.clone.clone.sunk | while | flops 619265 | bytes 824448 | solution.py:77
  27.0 0.7 fusion.393
  36.9 0.7 fusion.392
  51.6 0.1 constant_dynamic-update-slice_fusion.149
  51.8 0.1 constant_dynamic-update-slice_fusion.151
  52.1 0.1 constant_dynamic-update-slice_fusion.155
  52.3 0.1 constant_dynamic-update-slice_fusion.157
  52.9 0.1 constant_dynamic-update-slice_fusion.163
  53.5 0.1 constant_dynamic-update-slice_fusion.169
  54.0 0.1 constant_dynamic-update-slice_fusion.175
  56.0 0.7 fusion.393
  65.9 0.7 fusion.392
  80.3 0.1 constant_dynamic-update-slice_fusion.147
  80.9 0.1 constant_dynamic-update-slice_fusion.153
  81.5 0.1 constant_dynamic-update-slice_fusion.159
  82.1 0.1 constant_dynamic-update-slice_fusion.165
  82.3 0.1 constant_dynamic-update-slice_fusion.167
  82.6 0.1 constant_dynamic-update-slice_fusion.171
  82.8 0.1 constant_dynamic-update-slice_fusion.173
  85.0 0.7 fusion.393
  94.9 0.7 fusion.392
  109.5 0.1 constant_dynamic-update-slice_fusion.149
  109.7 0.1 constant_dynamic-update-slice_fusion.151
  110.1 0.1 constant_dynamic-update-slice_fusion.155
  110.3 0.1 constant_dynamic-update-slice_fusion.157
  110.6 0.1 constant_dynamic-update-slice_fusion.161
  110.8 0.1 constant_dynamic-update-slice_fusion.163
  111.4 0.1 constant_dynamic-update-slice_fusion.169
  112.0 0.1 constant_dynamic-update-slice_fusion.175
  113.9 0.7 fusion.393
  123.8 0.7 fusion.392
  138.3 0.1 constant_dynamic-update-slice_fusion.147
  138.8 0.1 constant_dynamic-update-slice_fusion.153
  142.8 0.2 copy.303
  143.0 0.3 convolution_convert_fusion.3
  143.3 0.9 copy.306
  144.2 6.0 %all-to-all-start.3 = ((bf16[1,128,8,128]{3,2,0,1:T(8,128)(2,1)}), bf16[1,128,8,128]{3,2,0,1:T(8,128)(2,1)S(1)}, u32[]{:S(2)}, u32[]{:S(2)}) async-start(bf16[1,128,8,128]{3,2,0,1:T(8,128)(2,1)} %copy.306), calls=%async_computation.3 | async-start | bytes 524288 | tf_op jit(solution)/shard_map/all_to_all | solution.py:121
  150.3 9.9 %all-to-all-done.3 = bf16[1,128,8,128]{3,2,0,1:T(8,128)(2,1)S(1)} async-done(((bf16[1,128,8,128]{3,2,0,1:T(8,128)(2,1)}), bf16[1,128,8,128]{3,2,0,1:T(8,128)(2,1)S(1)}, u32[]{:S(2)}, u32[]{:S(2)}) %all-to-all-start.3) | async-done | bytes 262176 | tf_op jit(solution)/shard_map/all_to_all | solution.py:121
  160.4 0.3 fusion.298
  161.1 12.7 %all_to_all.104 = bf16[16,1,8,8,128]{4,3,2,1,0:T(8,128)(2,1)S(1)} all-to-all(bf16[16,1,8,8,128]{4,3,2,1,0:T(8,128)(2,1)S(1)} %constant_dynamic-update-slice_fusion.64), channel_id=1, replica_groups=mesh['lon'=2,'lat'=16] {'lat'}, dimensions={0} | all-to-all | bytes 524288 | tf_op jit(solution)/shard_map/all_to_all | solution.py:129
  173.8 0.2 reshape.2625
  173.9 0.3 convolution_convert_fusion.2
  174.2 0.2 copy.310
  174.4 12.7 %all_to_all.105 = bf16[1,128,8,128]{3,2,0,1:T(8,128)(2,1)S(1)} all-to-all(bf16[1,128,8,128]{3,2,0,1:T(8,128)(2,1)S(1)} %copy.310), channel_id=1, replica_groups=mesh['lon'=2,'lat'=16] {'lat'}, dimensions={1} | all-to-all | bytes 524288 | tf_op jit(solution)/shard_map/all_to_all | solution.py:137
  187.1 0.8 copy.333
  187.9 3.4 %all-to-all-start.6 = ((bf16[1,8,1,128,128]{4,3,2,0,1:T(8,128)(2,1)}), bf16[1,8,1,128,128]{4,3,2,0,1:T(8,128)(2,1)S(1)}, u32[]{:S(2)}, u32[]{:S(2)}) async-start(bf16[1,8,1,128,128]{4,3,2,0,1:T(8,128)(2,1)} %bitcast.775), calls=%async_computation.6 | async-start | bytes 524288 | tf_op jit(solution)/shard_map/all_to_all | solution.py:139
  191.3 0.1 copy.294
  191.5 5.3 %all-to-all-done.6 = bf16[1,8,1,128,128]{4,3,2,0,1:T(8,128)(2,1)S(1)} async-done(((bf16[1,8,1,128,128]{4,3,2,0,1:T(8,128)(2,1)}), bf16[1,8,1,128,128]{4,3,2,0,1:T(8,128)(2,1)S(1)}, u32[]{:S(2)}, u32[]{:S(2)}) %all-to-all-start.6) | async-done | bytes 262176 | tf_op jit(solution)/shard_map/all_to_all | solution.py:139
  196.8 0.3 fusion.297
  197.1 0.2 copy.315
  197.3 7.6 %all_to_all.106 = bf16[1,4,256,128]{3,1,0,2:T(4,128)(2,1)S(1)} all-to-all(bf16[1,4,256,128]{3,1,0,2:T(4,128)(2,1)S(1)} %copy.315), channel_id=1, replica_groups=mesh['lon'=2,'lat'=16] {'lon'}, dimensions={2} | all-to-all | bytes 524288 | tf_op jit(solution)/shard_map/all_to_all | solution.py:146
  204.9 0.9 copy-done.2
  205.8 1.1 fusion.314
  (809 shorter events, 24.6 us)
Async XLA Ops:
  0.0 204.9 %copy-start = (bf16[128,128]{1,0:T(8,128)(2,1)S(1)}, bf16[128,128]{1,0:T(8,128)(2,1)}, u32[]{:S(2)}) copy-start(bf16[128,128]{1,0:T(8,128)(2,1)} %param.7) | copy-start | bytes 98308
  0.0 10.2 %all-to-all-start = ((bf16[1,8,128,128]{3,2,0,1:T(8,128)(2,1)}), bf16[1,8,128,128]{3,2,0,1:T(8,128)(2,1)S(1)}, u32[]{:S(2)}, u32[]{:S(2)}) async-start(bf16[1,8,128,128]{3,2,0,1:T(8,128)(2,1)} %bitcast.1245), calls=%async_computation | async-start | bytes 524288 | tf_op jit(solution)/shard_map/all_to_all | solution.py:105
  11.2 8.6 %all-to-all-start.1 = ((bf16[1,4,2,128,128]{4,3,1,0,2:T(8,128)(2,1)}), bf16[1,4,2,128,128]{4,3,1,0,2:T(8,128)(2,1)S(1)}, u32[]{:S(2)}, u32[]{:S(2)}) async-start(bf16[1,4,2,128,128]{4,3,1,0,2:T(8,128)(2,1)} %copy.300), calls=%async_computation.1 | async-start | bytes 524288 | tf_op jit(solution)/shard_map/all_to_all | solution.py:112
  20.7 122.1 %all-to-all-start.2 = ((bf16[1,8,128,128]{3,1,0,2:T(8,128)(2,1)}), bf16[1,8,128,128]{3,1,0,2:T(8,128)(2,1)S(1)}, u32[]{:S(2)}, u32[]{:S(2)}) async-start(bf16[1,8,128,128]{3,1,0,2:T(8,128)(2,1)} %copy.301), calls=%async_computation.2 | async-start | bytes 524288 | tf_op jit(solution)/shard_map/all_to_all | solution.py:114
  143.3 6.9 %copy-start.1 = (bf16[8,2,128,128]{3,2,1,0:T(8,128)(2,1)S(1)}, bf16[8,2,128,128]{3,2,1,0:T(8,128)(2,1)}, u32[]{:S(2)}) copy-start(bf16[8,2,128,128]{3,2,1,0:T(8,128)(2,1)} %param.6) | copy-start | bytes 1572868
  144.2 16.0 %all-to-all-start.3 = ((bf16[1,128,8,128]{3,2,0,1:T(8,128)(2,1)}), bf16[1,128,8,128]{3,2,0,1:T(8,128)(2,1)S(1)}, u32[]{:S(2)}, u32[]{:S(2)}) async-start(bf16[1,128,8,128]{3,2,0,1:T(8,128)(2,1)} %copy.306), calls=%async_computation.3 | async-start | bytes 524288 | tf_op jit(solution)/shard_map/all_to_all | solution.py:121
  187.9 9.0 %all-to-all-start.6 = ((bf16[1,8,1,128,128]{4,3,2,0,1:T(8,128)(2,1)}), bf16[1,8,1,128,128]{4,3,2,0,1:T(8,128)(2,1)S(1)}, u32[]{:S(2)}, u32[]{:S(2)}) async-start(bf16[1,8,1,128,128]{4,3,2,0,1:T(8,128)(2,1)} %bitcast.775), calls=%async_computation.6 | async-start | bytes 524288 | tf_op jit(solution)/shard_map/all_to_all | solution.py:139
  204.9 1.0 copy-start.2
